TPU v7x, 32 devices: a whole 2x2x4 slice. The times are simulated.
32 devices in a mesh: dp: 8 (over y, x, core), tensor: 4 (over z).
Axes of the slice: x: 2, y: 2, z: 4, core: 2. Of those that a mesh axis runs over, the one named last changes fastest.
Arguments:
- tokens: bfloat16 [16384, 1536], P('dp'), may hold values from -6 to 6
- lengths: int32 [8], P('dp'), may hold values from 1024 to 2048, as said below
- cotangent: bfloat16 [16384, 1536], P('dp'), may hold values from -6 to 6
- norm_gain: float32 [1536], replicated, may hold values from 0.1 to 1.9
- query_w: bfloat16 [1536, 1536], P(None, 'tensor'), may hold values from -0.15625 to 0.15625
- key_weight: bfloat16 [1536, 512], P(None, 'tensor'), may hold values from -0.15625 to 0.15625
- value_weight: bfloat16 [1536, 512], P(None, 'tensor'), may hold values from -0.15625 to 0.15625
- out_w: bfloat16 [1536, 1536], P('tensor'), may hold values from -0.625 to 0.625
- query_gain: float32 [64], replicated, may hold values from 0.1 to 1.9
- key_gain: float32 [64], replicated, may hold values from 0.1 to 1.9
- mlp_gain: float32 [1536], replicated, may hold values from 0.1 to 1.9
- gate_w: bfloat16 [1536, 6912], P(None, 'tensor'), may hold values from -0.15625 to 0.15625
- up_w: bfloat16 [1536, 6912], P(None, 'tensor'), may hold values from -0.15625 to 0.15625
- down_w: bfloat16 [6912, 1536], P('tensor'), may hold values from -0.078125 to 0.078125
Outputs:
- block_out: bfloat16 [16384, 1536], P('dp')
- input_grad: float32 [16384, 1536], P('dp')
- norm_gain_grad: float32 [1536], replicated
- query_w_grad: float32 [1536, 1536], P(None, 'tensor')
- key_w_grad: float32 [1536, 512], P(None, 'tensor')
- value_weight_gradient: float32 [1536, 512], P(None, 'tensor')
- out_w_grad: float32 [1536, 1536], P('tensor')
- query_gain_grad: float32 [64], replicated
- key_gain_grad: float32 [64], replicated
- mlp_gain_grad: float32 [1536], replicated
- gate_w_grad: float32 [1536, 6912], P(None, 'tensor')
- up_w_grad: float32 [1536, 6912], P(None, 'tensor')
- down_w_grad: float32 [6912, 1536], P('tensor')
Inputs may be any that keep to these rules, and one draw needn't show every extreme that they name: `lengths`: each sequence's live slots are its first ones; some sequence fills all 2048 slots.
All inputs are finite; a program needn't handle non-finite values.
Results may differ from a plain program's by a relative error of at most 0.024.
Values may be sent and summed in bfloat16 or wider, within the bound.
A program may use at most 384 MiB of HBM per device.

v0:
```python
import math
import jax
import jax.numpy as jnp
from jax import lax
from jax.sharding import PartitionSpec as P

HEAD_SIZE = 64
BLK = 512
EPSILON = 1e-05
ROPE_BASE = 1000000.0


def rms_scale(inputs, gain_vec):
    return (
        inputs * lax.rsqrt(jnp.mean(inputs * inputs, axis=-1, keepdims=True) + EPSILON) * gain_vec
    )


def rotary(inputs, head_count):
    row_count = inputs.shape[0]
    half_dim = HEAD_SIZE // 2
    positions = jnp.arange(row_count).astype(jnp.float32)[:, None]
    inv_freq = jnp.exp(
        jnp.arange(half_dim).astype(jnp.float32) * (-2.0 * math.log(ROPE_BASE) / HEAD_SIZE)
    )
    angles = positions * inv_freq[None, :]
    cosine = jnp.cos(angles)[:, None, :]
    sine_tab = jnp.sin(angles)[:, None, :]
    split_heads = inputs.reshape(row_count, head_count, HEAD_SIZE)
    lower_half = split_heads[..., :half_dim]
    upper_half = split_heads[..., half_dim:]
    turned = jnp.concatenate(
        [lower_half * cosine - upper_half * sine_tab, upper_half * cosine + lower_half * sine_tab],
        axis=-1,
    )
    return turned.reshape(row_count, head_count * HEAD_SIZE)


def head_norm(inputs, gain_vec, head_count):
    row_count = inputs.shape[0]
    return rms_scale(inputs.reshape(row_count, head_count, HEAD_SIZE), gain_vec).reshape(
        row_count, head_count * HEAD_SIZE
    )


def prepare(queries, keys_val, q_gain, k_gain):
    q_count = queries.shape[1] // HEAD_SIZE
    kv_count = keys_val.shape[1] // HEAD_SIZE
    return (
        rotary(head_norm(queries, q_gain, q_count), q_count),
        rotary(head_norm(keys_val, k_gain, kv_count), kv_count),
    )


def swiglu(gate_val, up_val):
    return gate_val * jax.nn.sigmoid(gate_val) * up_val


def left_dot(left, right):
    return lax.dot_general(
        left, right, (((0,), (0,)), ((), ())), preferred_element_type=jnp.float32
    )


def right_dot(left, right):
    return lax.dot_general(
        left, right, (((1,), (1,)), ((), ())), preferred_element_type=jnp.float32
    )


def masked_scores(q_block, k_block, first_row, length):
    raw_scores = jnp.einsum("kgqd,kjd->kgqj", q_block, k_block, preferred_element_type=jnp.float32)
    scaled = raw_scores * float(HEAD_SIZE) ** (-0.5)
    query_pos = first_row + jnp.arange(q_block.shape[2], dtype=jnp.int32)
    key_pos = jnp.arange(k_block.shape[1], dtype=jnp.int32)
    allowed = (key_pos[None, :] <= query_pos[:, None]) & (key_pos[None, :] < length)
    return jnp.where(allowed, scaled, -jnp.inf)


def on_device(
    tokens,
    lengths,
    cotangent,
    norm_gain,
    query_w,
    key_weight,
    value_weight,
    out_w,
    query_gain,
    key_gain,
    mlp_gain,
    gate_w,
    up_w,
    down_w,
):
    row_count = tokens.shape[0]
    length = lengths[0]
    live_rows = (jnp.arange(row_count, dtype=jnp.int32) < length).astype(jnp.float32)
    inputs = tokens.astype(jnp.float32)
    normed, norm_pull = jax.vjp(rms_scale, inputs, norm_gain)
    normed_b = normed.astype(jnp.bfloat16)
    queries = jnp.dot(normed_b, query_w, preferred_element_type=jnp.float32)
    keys_val = jnp.dot(normed_b, key_weight, preferred_element_type=jnp.float32)
    values_b = jnp.dot(normed_b, value_weight, preferred_element_type=jnp.float32).astype(
        jnp.bfloat16
    )
    (query_r, keys_r), prep_pull = jax.vjp(prepare, queries, keys_val, query_gain, key_gain)
    kv_count = key_weight.shape[1] // HEAD_SIZE
    group_size = query_w.shape[1] // key_weight.shape[1]
    q_heads = (
        query_r.astype(jnp.bfloat16)
        .reshape(row_count, kv_count, group_size, HEAD_SIZE)
        .transpose(1, 2, 0, 3)
    )
    k_heads = keys_r.astype(jnp.bfloat16).reshape(row_count, kv_count, HEAD_SIZE).transpose(1, 0, 2)
    v_heads = values_b.reshape(row_count, kv_count, HEAD_SIZE).transpose(1, 0, 2)
    block_outs = []
    log_sums = []
    for first_row in range(0, row_count, BLK):
        last_row = first_row + BLK
        scores = masked_scores(
            q_heads[:, :, first_row:last_row], k_heads[:, :last_row], first_row, length
        )
        row_max = jnp.max(scores, axis=-1, keepdims=True)
        weight = jnp.exp(scores - row_max)
        row_sum = jnp.sum(weight, axis=-1, keepdims=True)
        attn_prob = (weight / row_sum).astype(jnp.bfloat16)
        block_outs.append(
            jnp.einsum(
                "kgqj,kjd->kgqd",
                attn_prob,
                v_heads[:, :last_row],
                preferred_element_type=jnp.float32,
            )
        )
        log_sums.append(row_max + jnp.log(row_sum))
    mixed_b = (
        jnp.concatenate(block_outs, axis=2)
        .transpose(2, 0, 1, 3)
        .reshape(row_count, kv_count * group_size * HEAD_SIZE)
        .astype(jnp.bfloat16)
    )
    attn_out = lax.psum(
        jnp.dot(mixed_b, out_w, preferred_element_type=jnp.float32).astype(jnp.bfloat16), "tensor"
    ).astype(jnp.float32)
    residual = inputs + attn_out
    normed2, norm2_pull = jax.vjp(rms_scale, residual, mlp_gain)
    normed2_b = normed2.astype(jnp.bfloat16)
    gate_val = jnp.dot(normed2_b, gate_w, preferred_element_type=jnp.float32)
    up_val = jnp.dot(normed2_b, up_w, preferred_element_type=jnp.float32)
    hidden, glu_pull = jax.vjp(swiglu, gate_val, up_val)
    hidden_b = hidden.astype(jnp.bfloat16)
    mlp_out = lax.psum(
        jnp.dot(hidden_b, down_w, preferred_element_type=jnp.float32).astype(jnp.bfloat16), "tensor"
    ).astype(jnp.float32)
    block_out = (residual + mlp_out).astype(jnp.bfloat16)
    d_out = cotangent.astype(jnp.float32) * live_rows[:, None]
    d_out_b = d_out.astype(jnp.bfloat16)
    d_down = left_dot(hidden_b, d_out_b)
    d_hidden = right_dot(d_out_b, down_w)
    d_gate, d_up = glu_pull(d_hidden)
    d_gate_b = d_gate.astype(jnp.bfloat16)
    d_up_b = d_up.astype(jnp.bfloat16)
    d_gate_w = left_dot(normed2_b, d_gate_b)
    d_up_w = left_dot(normed2_b, d_up_b)
    d_normed2 = lax.psum(
        (right_dot(d_gate_b, gate_w) + right_dot(d_up_b, up_w)).astype(jnp.bfloat16), "tensor"
    ).astype(jnp.float32)
    d_resid_norm, d_mlp_gain = norm2_pull(d_normed2)
    d_resid = d_out + d_resid_norm
    d_resid_b = d_resid.astype(jnp.bfloat16)
    output_weight_cotangent = left_dot(mixed_b, d_resid_b)
    d_mixed = right_dot(d_resid_b, out_w).astype(jnp.bfloat16)
    d_heads = d_mixed.reshape(row_count, kv_count, group_size, HEAD_SIZE).transpose(1, 2, 0, 3)
    d_keys = jnp.zeros((kv_count, row_count, HEAD_SIZE), jnp.float32)
    d_values = jnp.zeros((kv_count, row_count, HEAD_SIZE), jnp.float32)
    d_queries = []
    for block_idx in range(row_count // BLK):
        first_row = block_idx * BLK
        last_row = first_row + BLK
        q_block = q_heads[:, :, first_row:last_row]
        scores = masked_scores(q_block, k_heads[:, :last_row], first_row, length)
        attn_prob = jnp.exp(scores - log_sums[block_idx])
        d_block = d_heads[:, :, first_row:last_row]
        d_values = d_values.at[:, :last_row].add(
            jnp.einsum(
                "kgqj,kgqd->kjd",
                attn_prob.astype(jnp.bfloat16),
                d_block,
                preferred_element_type=jnp.float32,
            )
        )
        d_prob = jnp.einsum(
            "kgqd,kjd->kgqj", d_block, v_heads[:, :last_row], preferred_element_type=jnp.float32
        )
        spread = jnp.sum(attn_prob * d_prob, axis=-1, keepdims=True)
        d_scores = (attn_prob * (d_prob - spread) * float(HEAD_SIZE) ** (-0.5)).astype(jnp.bfloat16)
        d_queries.append(
            jnp.einsum(
                "kgqj,kjd->kgqd",
                d_scores,
                k_heads[:, :last_row],
                preferred_element_type=jnp.float32,
            )
        )
        d_keys = d_keys.at[:, :last_row].add(
            jnp.einsum("kgqj,kgqd->kjd", d_scores, q_block, preferred_element_type=jnp.float32)
        )
    d_query_r = (
        jnp.concatenate(d_queries, axis=2)
        .transpose(2, 0, 1, 3)
        .reshape(row_count, kv_count * group_size * HEAD_SIZE)
    )
    d_keys_r = d_keys.transpose(1, 0, 2).reshape(row_count, kv_count * HEAD_SIZE)
    d_values_b = (
        d_values.transpose(1, 0, 2).reshape(row_count, kv_count * HEAD_SIZE).astype(jnp.bfloat16)
    )
    d_query_f, d_keys_f, d_qgain, d_kgain = prep_pull((d_query_r, d_keys_r))
    d_query_b = d_query_f.astype(jnp.bfloat16)
    d_keys_b = d_keys_f.astype(jnp.bfloat16)
    d_query_w = left_dot(normed_b, d_query_b)
    d_key_w = left_dot(normed_b, d_keys_b)
    d_value_w = left_dot(normed_b, d_values_b)
    d_normed = lax.psum(
        (
            right_dot(d_query_b, query_w)
            + right_dot(d_keys_b, key_weight)
            + right_dot(d_values_b, value_weight)
        ).astype(jnp.bfloat16),
        "tensor",
    ).astype(jnp.float32)
    d_input_norm, norm_gain_cotangent = norm_pull(d_normed)
    d_inputs = d_resid + d_input_norm
    head_totals = lax.psum((d_qgain, d_kgain), ("dp", "tensor"))
    all_totals = (
        lax.psum(norm_gain_cotangent.astype(jnp.bfloat16), "dp").astype(jnp.float32),
        lax.psum(d_query_w.astype(jnp.bfloat16), "dp").astype(jnp.float32),
        lax.psum(d_key_w.astype(jnp.bfloat16), "dp").astype(jnp.float32),
        lax.psum(d_value_w.astype(jnp.bfloat16), "dp").astype(jnp.float32),
        lax.psum(output_weight_cotangent.astype(jnp.bfloat16), "dp").astype(jnp.float32),
        lax.psum(d_gate_w.astype(jnp.bfloat16), "dp").astype(jnp.float32),
        lax.psum(d_up_w.astype(jnp.bfloat16), "dp").astype(jnp.float32),
        lax.psum(d_down.astype(jnp.bfloat16), "dp").astype(jnp.float32),
        lax.psum(d_mlp_gain.astype(jnp.bfloat16), "dp").astype(jnp.float32),
    )
    g_norm, g_query, g_key, g_value, g_out, g_gate, g_up, g_down, g_mlp = all_totals
    return (
        block_out,
        d_inputs,
        g_norm,
        g_query,
        g_key,
        g_value,
        g_out,
        head_totals[0],
        head_totals[1],
        g_mlp,
        g_gate,
        g_up,
        g_down,
    )


def solution(mesh):
    return jax.shard_map(
        on_device,
        mesh=mesh,
        in_specs=(
            P("dp", None),
            P("dp"),
            P("dp", None),
            P(),
            P(None, "tensor"),
            P(None, "tensor"),
            P(None, "tensor"),
            P("tensor", None),
            P(),
            P(),
            P(),
            P(None, "tensor"),
            P(None, "tensor"),
            P("tensor", None),
        ),
        out_specs=(
            P("dp", None),
            P("dp", None),
            P(),
            P(None, "tensor"),
            P(None, "tensor"),
            P(None, "tensor"),
            P("tensor", None),
            P(),
            P(),
            P(),
            P(None, "tensor"),
            P(None, "tensor"),
            P("tensor", None),
        ),
        check_vma=False,
    )
```

profile of v0, /device:TPU:0, one launch (start us, length us, event | category | flops | bytes accessed | tf_op | source)
XLA Modules:
  0.0 1743.3 jit_solution(18047508188142419568)
XLA Ops:
  116.9 223.2 %all-reduce.15.cloned.1.call-done = bf16[2048,1536]{1,0:T(8,128)(2,1)} async-done(((bf16[2048,1536]{1,0:T(8,128)(2,1)}), bf16[2048,1536]{1,0:T(8,128)(2,1)}) %all-reduce.15.cloned.1.call-update) | async-done | bytes 6291472 | tf_op jit(solution)/shard_map/psum | solution.py:143
  353.2 16.7 fusion.282
  369.9 13.7 fusion.281
  383.6 28.7 %multiply_convert_fusion.2 = (bf16[2048,1728]{0,1:T(8,128)(2,1)}, bf16[2048,1728]{0,1:T(8,128)(2,1)}, bf16[2048,1728]{0,1:T(8,128)(2,1)}) fusion(f32[2048,1728]{0,1:T(8,128)} %fusion.281, f32[2048,1728]{0,1:T(8,128)} %fusion.282, bf16[1728,1536]{1,0:T(8,128)(2,1)} %param.47, bf16[2048,1536]{1,0:T(8,128)(2,1)} %param.36, f32[2048]{0:T(1024)S(1)} %fusion.239), kind=kOutput, calls=%fused_computation.41 | convolution fusion | flops 10937696256 | bytes 61153280 | tf_op jit(solution)/shard_map/dot_general | solution.py:66
  412.3 16.5 fusion.283
  428.8 17.7 %add_convert_fusion.1 = bf16[2048,1536]{1,0:T(8,128)(2,1)} fusion(f32[2048,1536]{1,0:T(8,128)S(1)} %fusion.283, bf16[2048,1728]{0,1:T(8,128)(2,1)} %get-tuple-element.146, bf16[1536,1728]{0,1:T(8,128)(2,1)} %param.46), kind=kOutput, calls=%fused_computation.63 | convolution fusion | flops 10877927424 | bytes 31260672 | tf_op jit(solution)/shard_map/dot_general | solution.py:66
  446.5 17.0 convolution_convert_fusion
  463.5 16.9 convolution_convert_fusion.1
  480.4 13.3 convolution_convert_fusion.2
  493.8 174.6 %all-reduce.17.cloned.1.call-done = bf16[2048,1536]{1,0:T(8,128)(2,1)} async-done(((bf16[2048,1536]{1,0:T(8,128)(2,1)}), bf16[2048,1536]{1,0:T(8,128)(2,1)}) %all-reduce.17.cloned.1.call-update) | async-done | bytes 6291472 | tf_op jit(solution)/shard_map/psum | solution.py:166
  715.0 12.1 fusion.116
  780.0 33.9 %fusion.84 = f32[2,3,512,64]{2,3,1,0:T(8,128)} fusion(f32[2,3,512,1024]{3,2,1,0:T(8,128)} %fusion.220, f32[2,3,512,1024]{3,2,1,0:T(8,128)} %copy-done.11, f32[2,3,512]{2,1,0:T(4,128)S(1)} %copy-done.79, pred[512,1024]{1,0:T(8,128)(4,1)} %copy-done.22, bf16[2,2048,64]{1,2,0:T(8,128)(2,1)S(1)} %copy-done.47), kind=kOutput, calls=%fused_computation.99 | convolution fusion | flops 437260288 | bytes 52461568 | tf_op jit(solution)/shard_map/kgqj,kjd->kgqd/dot_general | solution.py:199
  813.9 34.6 %fusion.193 = f32[2,2048,64]{1,2,0:T(8,128)} fusion(f32[2,2048,64]{1,2,0:T(8,128)} %scatter-add.20, f32[2,3,512,1024]{3,2,1,0:T(8,128)} %fusion.220, f32[2,3,512,1024]{3,2,1,0:T(8,128)} %copy-done.11, f32[2,3,512]{2,1,0:T(4,128)S(1)} %copy-done.79, pred[512,1024]{1,0:T(8,128)(4,1)} %copy-done.22, bf16[2,3,2048,64]{2,3,1,0:T(8,128)(2,1)S(1)} %bitcast.225), kind=kOutput, calls=%fused_computation.180 | convolution fusion | flops 437391360 | bytes 52854784 | tf_op jit(solution)/shard_map/kgqj,kgqd->kjd/dot_general | solution.py:207
  848.5 29.6 %fusion.63 = f32[2,3,512,64]{2,3,1,0:T(8,128)} fusion(f32[2,3,512,1536]{3,2,1,0:T(8,128)} %fusion.217, f32[2,3,512,1536]{3,2,1,0:T(8,128)} %get-tuple-element.166, f32[2,3,512]{2,1,0:T(4,128)S(1)} %copy-done.77, bf16[2,2048,64]{1,2,0:T(8,128)(2,1)S(1)} %copy-done.47), kind=kOutput, calls=%fused_computation.82 | convolution fusion | flops 637014528 | bytes 76709888 | tf_op jit(solution)/shard_map/kgqj,kjd->kgqd/dot_general | solution.py:199
  878.1 30.0 %fusion.167 = f32[2,2048,64]{1,2,0:T(8,128)} fusion(f32[2,2048,64]{1,2,0:T(8,128)} %fusion.193, f32[2,3,512,1536]{3,2,1,0:T(8,128)} %fusion.217, f32[2,3,512,1536]{3,2,1,0:T(8,128)} %get-tuple-element.166, f32[2,3,512]{2,1,0:T(4,128)S(1)} %copy-done.77, bf16[2,3,2048,64]{2,3,1,0:T(8,128)(2,1)S(1)} %bitcast.226), kind=kOutput, calls=%fused_computation.157 | convolution fusion | flops 637211136 | bytes 77496320 | tf_op jit(solution)/shard_map/kgqj,kgqd->kjd/dot_general | solution.py:207
  908.2 45.0 %fusion.27 = f32[2,3,512,64]{2,3,1,0:T(8,128)} fusion(f32[2,3,512,2048]{3,2,1,0:T(8,128)} %fusion.214, f32[2,3,512,2048]{3,2,1,0:T(8,128)} %get-tuple-element.164, f32[2,3,512]{2,1,0:T(4,128)S(1)} %copy-done.78, pred[512,2048]{1,0:T(8,128)(4,1)} %copy-done.20, bf16[2048,2,32]{0,2,1:T(8,128)(2,1)S(1)} %copy-done.41, bf16[2048,2,32]{0,2,1:T(8,128)(2,1)S(1)} %copy-done.38), kind=kOutput, calls=%fused_computation.47 | convolution fusion | flops 875566080 | bytes 52703232 | tf_op jit(solution)/shard_map/kgqj,kjd->kgqd/dot_general | solution.py:199
  953.2 48.7 %fusion.173 = f32[2048,2,64]{0,2,1:T(8,128)} fusion(f32[2,2048,64]{1,2,0:T(8,128)} %fusion.167, f32[2,3,512,2048]{3,2,1,0:T(8,128)} %fusion.214, f32[2,3,512,2048]{3,2,1,0:T(8,128)} %get-tuple-element.164, f32[2,3,512]{2,1,0:T(4,128)S(1)} %copy-done.78, pred[512,2048]{1,0:T(8,128)(4,1)} %copy-done.20, bf16[2,3,2048,64]{2,3,1,0:T(8,128)(2,1)S(1)} %bitcast.227), kind=kOutput, calls=%fused_computation.159 | convolution fusion | flops 874779648 | bytes 105283584 | tf_op jit(solution)/shard_map/kgqj,kgqd->kjd/dot_general | solution.py:207
  1016.6 17.4 convolution_convert_fusion.3
  1047.0 13.2 add_convert_fusion
  1060.3 40.8 %all-reduce.6 = (f32[64]{0:T(128)}, f32[64]{0:T(128)}) all-reduce(f32[64]{0:T(128)S(1)} %get-tuple-element.129, f32[64]{0:T(128)S(1)} %get-tuple-element.131), channel_id=1, replica_groups=mesh['dp'=8,'tensor'=4] {'dp','tensor'}, use_global_device_ids=true, to_apply=%region_31.32 | all-reduce | flops 128 | bytes 1024 | tf_op jit(solution)/shard_map/psum | solution.py:234
  1101.1 160.8 %all-reduce.19.cloned.1.call-done = (bf16[1536,384]{1,0:T(8,128)(2,1)}, bf16[1536,128]{1,0:T(8,128)(2,1)}, bf16[1536,128]{1,0:T(8,128)(2,1)}, bf16[384,1536]{1,0...) async-done(((bf16[1536,384]{1,0:T(8,128)(2,1)}, bf16[1536,128]{1,0:T(8,128)(2,1)}, bf16[1536,128]{1,0:T(8,128)(2,1)}, ...) | async-done | bytes 19070992 | tf_op jit(solution)/shard_map/psum | solution.py:237
  1288.8 403.2 %all-reduce.21.cloned.1.call-done = (bf16[2048,1536]{1,0:T(8,128)(2,1)}, bf16[2048,1536]{1,0:T(8,128)(2,1)}) async-done(((bf16[2048,1536]{1,0:T(8,128)(2,1)}, bf16[2048,1536]{1,0:T(8,128)(2,1)}), (bf16[2048,1536]{1,0:T(8,128)(2,1)}, bf16[2048,1536]{1,0:T(8,128)(2,1)})) %all-reduce.21.cloned.1.call-update) | async-done | bytes 12582928 | tf_op jit(solution)/shard_map/psum | solution.py:153
  1700.2 13.9 all-reduce.7
  1715.4 20.9 %fusion.34 = (f32[2048,1536]{1,0:T(8,128)}, bf16[2048,1536]{1,0:T(8,128)(2,1)}) fusion(f32[2048,1536]{1,0:T(8,128)} %copy-done.6, bf16[2048,1536]{1,0:T(8,128)(2,1)} %get-tuple-element.145, bf16[2048,1536]{1,0:T(8,128)(2,1)} %param.34, f32[2048]{0:T(1024)S(1)} %multiply_multiply_fusion.4, f32[1536]{0:T(1024)S(1)} %copy-done.59, f32[2048]{0:T(1024)S(1)} %copy-done.56, ...), kind=kLoop, calls=%fused_computation.53 | loop fusion | flops 40894464 | bytes 56645632 | tf_op jit(solution)/shard_map/add | solution.py:233
  (321 shorter events, 284.1 us)
Async XLA Ops:
  7.2 101.7 %copy-start = (bf16[384,1536]{1,0:T(8,128)(2,1)S(1)}, bf16[384,1536]{1,0:T(8,128)(2,1)}, u32[]{:S(2)}) copy-start(bf16[384,1536]{1,0:T(8,128)(2,1)} %param.41) | copy-start | bytes 3538948
  7.2 332.9 %all-reduce.15.cloned.1.call-start = ((), (), s32[]{:S(2)}) async-start(), calls=%async_computation | async-start | bytes 12582912 | tf_op jit(solution)/shard_map/psum | solution.py:143
  19.2 76.7 %copy-start.12 = (bf16[2048,128]{0,1:T(8,128)(2,1)}, bf16[2048,128]{0,1:T(8,128)(2,1)S(1)}, u32[]{:S(2)}) copy-start(bf16[2048,128]{0,1:T(8,128)(2,1)S(1)} %convolution_convert_fusion.6) | copy-start | bytes 1572868
  27.7 45.6 %copy-start.37 = (bf16[2048,2,32]{0,2,1:T(8,128)(2,1)}, bf16[2048,2,32]{0,2,1:T(8,128)(2,1)S(1)}, u32[]{:S(2)}) copy-start(bf16[2048,2,32]{0,2,1:T(8,128)(2,1)S(1)} %get-tuple-element.157) | copy-start | bytes 786436
  28.8 44.5 %copy-start.28 = (bf16[2048,6,64]{0,2,1:T(8,128)(2,1)}, bf16[2048,6,64]{0,2,1:T(8,128)(2,1)S(1)}, u32[]{:S(2)}) copy-start(bf16[2048,6,64]{0,2,1:T(8,128)(2,1)S(1)} %pad_maximum_fusion.1) | copy-start | bytes 4718596
  73.4 22.5 %copy-start.20 = (pred[512,2048]{1,0:T(8,128)(4,1)}, pred[512,2048]{1,0:T(8,128)(4,1)S(1)}, u32[]{:S(2)}) copy-start(pred[512,2048]{1,0:T(8,128)(4,1)S(1)} %fusion.111) | copy-start | bytes 3145732
  114.4 233.2 %copy-start.64 = (f32[1536]{0:T(1024)S(1)}, f32[1536]{0:T(1024)}, u32[]{:S(2)}) copy-start(f32[1536]{0:T(1024)} %param.44) | copy-start | bytes 18436
  114.4 554.0 %all-reduce.17.cloned.1.call-start = ((), (), s32[]{:S(2)}) async-start(), calls=%async_computation.1 | async-start | bytes 12582912 | tf_op jit(solution)/shard_map/psum | solution.py:166
  446.4 815.5 %all-reduce.19.cloned.1.call-start = ((), (), s32[]{:S(2)}) async-start(), calls=%async_computation.2 | async-start | bytes 38141952 | tf_op jit(solution)/shard_map/psum | solution.py:237
  446.5 33.9 %slice-start.9 = ((s8[6291456]{0:T(1024)(128)(4,1)}), s8[4194304]{0:T(1024)(128)(4,1)S(1)}, s32[]{:S(2)}) async-start(s8[6291456]{0:T(1024)(128)(4,1)} %bitcast.204), calls=%async_computation.13 | async-start | bytes 8388608
  446.5 33.9 %slice-start.17 = ((s8[7077888]{0:T(1024)(128)(4,1)}), s8[4194304]{0:T(1024)(128)(4,1)S(1)}, s32[]{:S(2)}) async-start(s8[7077888]{0:T(1024)(128)(4,1)} %bitcast.234), calls=%async_computation.21 | async-start | bytes 8388608
  480.4 188.0 %copy-start.58 = (f32[2048]{0:T(1024)S(1)}, f32[2048]{0:T(1024)}, u32[]{:S(2)}) copy-start(f32[2048]{0:T(1024)} %copy-done.57) | copy-start | bytes 24580
  480.4 188.0 %copy-start.65 = (f32[1536]{0:T(1024)S(1)}, f32[1536]{0:T(1024)}, u32[]{:S(2)}) copy-start(f32[1536]{0:T(1024)} %param.44) | copy-start | bytes 18436
  493.8 185.0 %copy-start.63 = (f32[2048]{0:T(1024)S(1)}, f32[2048]{0:T(1024)}, u32[]{:S(2)}) copy-start(f32[2048]{0:T(1024)} %copy-done.62) | copy-start | bytes 24580
  780.0 33.9 %copy-start.29 = (bf16[2048,6,64]{0,2,1:T(8,128)(2,1)S(1)}, bf16[2048,6,64]{0,2,1:T(8,128)(2,1)}, u32[]{:S(2)}) copy-start(bf16[2048,6,64]{0,2,1:T(8,128)(2,1)} %copy-done.28) | copy-start | bytes 4718596
  878.1 30.0 %copy-start.38 = (bf16[2048,2,32]{0,2,1:T(8,128)(2,1)S(1)}, bf16[2048,2,32]{0,2,1:T(8,128)(2,1)}, u32[]{:S(2)}) copy-start(bf16[2048,2,32]{0,2,1:T(8,128)(2,1)} %copy-done.37) | copy-start | bytes 786436
  878.1 30.0 %copy-start.41 = (bf16[2048,2,32]{0,2,1:T(8,128)(2,1)S(1)}, bf16[2048,2,32]{0,2,1:T(8,128)(2,1)}, u32[]{:S(2)}) copy-start(bf16[2048,2,32]{0,2,1:T(8,128)(2,1)} %copy-done.39) | copy-start | bytes 786436
  953.2 51.1 %copy-start.15 = (f32[2048,32]{0,1:T(8,128)S(1)}, f32[2048,32]{0,1:T(8,128)}, u32[]{:S(2)}) copy-start(f32[2048,32]{0,1:T(8,128)} %copy-done.14) | copy-start | bytes 786436
  953.2 51.1 %copy-start.17 = (f32[2048,32]{0,1:T(8,128)S(1)}, f32[2048,32]{0,1:T(8,128)}, u32[]{:S(2)}) copy-start(f32[2048,32]{0,1:T(8,128)} %copy-done.16) | copy-start | bytes 786436
  1016.5 675.5 %all-reduce.21.cloned.1.call-start = ((), (), s32[]{:S(2)}) async-start(), calls=%async_computation.3 | async-start | bytes 25165824 | tf_op jit(solution)/shard_map/psum | solution.py:153
  1283.2 408.8 %copy-start.56 = (f32[2048]{0:T(1024)S(1)}, f32[2048]{0:T(1024)}, u32[]{:S(2)}) copy-start(f32[2048]{0:T(1024)} %copy-done.55) | copy-start | bytes 24580
  1283.2 408.8 %copy-start.59 = (f32[1536]{0:T(1024)S(1)}, f32[1536]{0:T(1024)}, u32[]{:S(2)}) copy-start(f32[1536]{0:T(1024)} %param.37) | copy-start | bytes 18436
  1288.8 411.4 %copy-start.61 = (f32[2048]{0:T(1024)S(1)}, f32[2048]{0:T(1024)}, u32[]{:S(2)}) copy-start(f32[2048]{0:T(1024)} %copy-done.60) | copy-start | bytes 24580
  1288.8 411.4 %copy-start.80 = (bf16[1536]{0:T(1024)(128)(2,1)S(1)}, bf16[1536]{0:T(1024)(128)(2,1)}, u32[]{:S(2)}) copy-start(bf16[1536]{0:T(1024)(128)(2,1)} %get-tuple-element.125) | copy-start | bytes 9220
  (86 other events, 604.9 us)
Sparse Core Ops, SparseCore 0:
  114.5 225.5 all-reduce.14
  446.6 221.7 all-reduce.16
  1016.6 245.2 all-reduce.18
  1265.0 426.9 all-reduce.20
where the time goes:
time: 1750 us; the launch traced here: 1740 us
  waiting for transfers between devices  962 us (55%)
  matrix products  563 us (32%)
  other arithmetic  137 us (8%)
  blocking collectives  54.8 us (3%)
    psum x1, waiting for transfers between devices, on_device(): lax.psum(jnp.dot(hidden_b, down_w, preferred_element_type=jnp.float32).as...  403 us
    psum x1, waiting for transfers between devices, on_device(): lax.psum(jnp.dot(mixed_b, out_w, preferred_element_type=jnp.float32).asty...  223 us
    psum x1, waiting for transfers between devices, on_device(): lax.psum((right_dot(d_gate_b, gate_w) + right_dot(d_up_b, up_w)).astype(j...  175 us
    psum x1, waiting for transfers between devices, on_device(): lax.psum(d_query_w.astype(jnp.bfloat16), 'dp').astype(jnp.float32)  161 us
    dot_general x4, matrix products, on_device(): jnp.einsum('kgqj,kgqd->kjd', d_scores, q_block, preferred_element_type=jn...  125 us
    dot_general x4, matrix products, on_device(): jnp.einsum('kgqj,kjd->kgqd', d_scores, k_heads[:, :last_row], preferred_e...  121 us
    dot_general x7, matrix products, right_dot(): lax.dot_general(left, right, (((1,), (1,)), ((), ())), preferred_element_...  91.9 us
    dot_general x7, matrix products, left_dot(): lax.dot_general(left, right, (((0,), (0,)), ((), ())), preferred_element_...  60.6 us
  transfers between devices with their start and end apart: 4, of which 4 were waited for; matrix products, arithmetic and copies ran while one was open for 7% of the time, Pallas kernels for 0%

commit v1 on v0

--- a/solution.py
+++ b/solution.py
@@ -234,7 +234,7 @@
     head_totals = lax.psum((d_qgain, d_kgain), ("dp", "tensor"))
     all_totals = (
         lax.psum(norm_gain_cotangent.astype(jnp.bfloat16), "dp").astype(jnp.float32),
-        lax.psum(d_query_w.astype(jnp.bfloat16), "dp").astype(jnp.float32),
+        jnp.sum(lax.all_gather(d_query_w.astype(jnp.bfloat16), "dp"), axis=0).astype(jnp.float32),
         lax.psum(d_key_w.astype(jnp.bfloat16), "dp").astype(jnp.float32),
         lax.psum(d_value_w.astype(jnp.bfloat16), "dp").astype(jnp.float32),
         lax.psum(output_weight_cotangent.astype(jnp.bfloat16), "dp").astype(jnp.float32),

time: 1750 us -> 1630 us (0.931)
  waiting for transfers between devices: 962 us -> 832 us
    psum x1, waiting for transfers between devices: 161 us -> 12.7 us  [on_device(): lax.psum(d_key_w.astype(jnp.bfloat16), 'dp').astype(jnp.float32)]
  transfers between devices with their start and end apart: 4 -> 5, of which waited for: 4 -> 5; matrix products, arithmetic and copies ran while one was open for 7% -> 17% of each run, Pallas kernels for 0% -> 0%
where the time goes in v1:
time: 1630 us; the launch traced here: 1620 us
  waiting for transfers between devices  832 us (51%)
  matrix products  564 us (35%)
  other arithmetic  143 us (9%)
  blocking collectives  55 us (3%)
  between operations  16.7 us (1%)
    psum x1, waiting for transfers between devices, on_device(): lax.psum(jnp.dot(hidden_b, down_w, preferred_element_type=jnp.float32).as...  406 us
    psum x1, waiting for transfers between devices, on_device(): lax.psum(jnp.dot(mixed_b, out_w, preferred_element_type=jnp.float32).asty...  223 us
    psum x1, waiting for transfers between devices, on_device(): lax.psum((right_dot(d_gate_b, gate_w) + right_dot(d_up_b, up_w)).astype(j...  175 us
    dot_general x4, matrix products, on_device(): jnp.einsum('kgqj,kjd->kgqd', d_scores, k_heads[:, :last_row], preferred_e...  123 us
    dot_general x4, matrix products, on_device(): jnp.einsum('kgqj,kgqd->kjd', d_scores, q_block, preferred_element_type=jn...  118 us
    dot_general x7, matrix products, right_dot(): lax.dot_general(left, right, (((1,), (1,)), ((), ())), preferred_element_...  91.3 us
    dot_general x7, matrix products, left_dot(): lax.dot_general(left, right, (((0,), (0,)), ((), ())), preferred_element_...  66.9 us
    psum x1, blocking collectives, on_device(): head_totals = lax.psum((d_qgain, d_kgain), ('dp', 'tensor'))  40.1 us
  transfers between devices with their start and end apart: 5, of which 5 were waited for; matrix products, arithmetic and copies ran while one was open for 17% of the time, Pallas kernels for 0%

profile of v1, /device:TPU:0, one launch (start us, length us, event | category | flops | bytes accessed | tf_op | source)
XLA Modules:
  0.0 1619.2 jit_solution(13675303825422726870)
XLA Ops:
  117.1 223.2 %all-reduce.15.cloned.1.call-done = bf16[2048,1536]{1,0:T(8,128)(2,1)} async-done(((bf16[2048,1536]{1,0:T(8,128)(2,1)}), bf16[2048,1536]{1,0:T(8,128)(2,1)}) %all-reduce.15.cloned.1.call-update) | async-done | bytes 6291472 | tf_op jit(solution)/shard_map/psum | solution.py:143
  353.3 16.7 %fusion.282 = f32[2048,1728]{0,1:T(8,128)} fusion(bf16[2048,1536]{1,0:T(8,128)(2,1)S(1)} %multiply_convert_fusion.5, bf16[1536,1728]{0,1:T(8,128)(2,1)} %param.46), kind=kOutput, calls=%fused_computation.291 | convolution fusion | flops 10871635968 | bytes 25755648 | tf_op jit(solution)/shard_map/dot_general | solution.py:150
  370.1 13.7 fusion.281
  383.8 28.7 %multiply_convert_fusion.2 = (bf16[2048,1728]{0,1:T(8,128)(2,1)}, bf16[2048,1728]{0,1:T(8,128)(2,1)}, bf16[2048,1728]{0,1:T(8,128)(2,1)}) fusion(f32[2048,1728]{0,1:T(8,128)} %fusion.281, f32[2048,1728]{0,1:T(8,128)} %fusion.282, bf16[1728,1536]{1,0:T(8,128)(2,1)} %param.47, bf16[2048,1536]{1,0:T(8,128)(2,1)} %param.36, f32[2048]{0:T(1024)S(1)} %fusion.239), kind=kOutput, calls=%fused_computation.41 | convolution fusion | flops 10937696256 | bytes 61153280 | tf_op jit(solution)/shard_map/dot_general | solution.py:66
  412.5 16.5 %fusion.283 = f32[2048,1536]{1,0:T(8,128)S(1)} fusion(bf16[2048,1728]{0,1:T(8,128)(2,1)} %get-tuple-element.146, bf16[1536,1728]{0,1:T(8,128)(2,1)} %param.45), kind=kOutput, calls=%fused_computation.292 | convolution fusion | flops 10871635968 | bytes 24969216 | tf_op jit(solution)/shard_map/dot_general | solution.py:66
  428.9 17.7 %add_convert_fusion.1 = bf16[2048,1536]{1,0:T(8,128)(2,1)} fusion(f32[2048,1536]{1,0:T(8,128)S(1)} %fusion.283, bf16[2048,1728]{0,1:T(8,128)(2,1)} %get-tuple-element.145, bf16[1536,1728]{0,1:T(8,128)(2,1)} %param.46), kind=kOutput, calls=%fused_computation.63 | convolution fusion | flops 10877927424 | bytes 31260672 | tf_op jit(solution)/shard_map/dot_general | solution.py:66
  446.7 17.0 %convolution_convert_fusion = bf16[1536,1728]{0,1:T(8,128)(2,1)} fusion(bf16[2048,1728]{0,1:T(8,128)(2,1)} %get-tuple-element.145, bf16[2048,1536]{1,0:T(8,128)(2,1)} %copy-done.18), kind=kOutput, calls=%fused_computation.92 | convolution fusion | flops 10874290176 | bytes 18677760 | tf_op jit(solution)/shard_map/dot_general | solution.py:60
  463.7 16.8 %convolution_convert_fusion.1 = bf16[1536,1728]{0,1:T(8,128)(2,1)} fusion(bf16[2048,1728]{0,1:T(8,128)(2,1)} %get-tuple-element.146, bf16[2048,1536]{1,0:T(8,128)(2,1)} %copy-done.18), kind=kOutput, calls=%fused_computation.93 | convolution fusion | flops 10874290176 | bytes 18677760 | tf_op jit(solution)/shard_map/dot_general | solution.py:60
  480.6 13.3 convolution_convert_fusion.2
  493.9 174.6 %all-reduce.17.cloned.1.call-done = bf16[2048,1536]{1,0:T(8,128)(2,1)} async-done(((bf16[2048,1536]{1,0:T(8,128)(2,1)}), bf16[2048,1536]{1,0:T(8,128)(2,1)}) %all-reduce.17.cloned.1.call-update) | async-done | bytes 6291472 | tf_op jit(solution)/shard_map/psum | solution.py:166
  768.1 27.3 %fusion.193 = f32[2,2048,64]{1,2,0:T(8,128)} fusion(f32[2,2048,64]{1,2,0:T(8,128)} %scatter-add.20, f32[2,3,512,1024]{3,2,1,0:T(8,128)} %fusion.220, f32[2,3,512,1024]{3,2,1,0:T(8,128)} %copy-done.11, f32[2,3,512]{2,1,0:T(4,128)} %log_add_fusion.2, pred[512,1024]{1,0:T(8,128)(4,1)S(1)} %copy-done.23, bf16[2,3,2048,64]{2,3,1,0:T(8,128)(2,1)S(1)} %bitcast.226), kind=kOutput, calls=%fused_computation.180 | convolution fusion | flops 437391360 | bytes 52854784 | tf_op jit(solution)/shard_map/kgqj,kgqd->kjd/dot_general | solution.py:207
  795.4 30.1 %fusion.167 = f32[2,2048,64]{1,2,0:T(8,128)} fusion(f32[2,2048,64]{1,2,0:T(8,128)} %fusion.193, f32[2,3,512,1536]{3,2,1,0:T(8,128)} %fusion.217, f32[2,3,512,1536]{3,2,1,0:T(8,128)} %get-tuple-element.165, f32[2,3,512]{2,1,0:T(4,128)S(1)} %copy-done.76, bf16[2,3,2048,64]{2,3,1,0:T(8,128)(2,1)S(1)} %bitcast.227), kind=kOutput, calls=%fused_computation.157 | convolution fusion | flops 637211136 | bytes 77496320 | tf_op jit(solution)/shard_map/kgqj,kgqd->kjd/dot_general | solution.py:207
  825.5 48.8 %fusion.173 = f32[2048,2,64]{0,2,1:T(8,128)} fusion(f32[2,2048,64]{1,2,0:T(8,128)} %fusion.167, f32[2,3,512,2048]{3,2,1,0:T(8,128)} %fusion.214, f32[2,3,512,2048]{3,2,1,0:T(8,128)} %get-tuple-element.163, f32[2,3,512]{2,1,0:T(4,128)S(1)} %copy-done.78, pred[512,2048]{1,0:T(8,128)(4,1)} %copy-done.20, bf16[2,3,2048,64]{2,3,1,0:T(8,128)(2,1)} %bitcast.224), kind=kOutput, calls=%fused_computation.159 | convolution fusion | flops 874779648 | bytes 105283584 | tf_op jit(solution)/shard_map/kgqj,kgqd->kjd/dot_general | solution.py:207
  881.9 17.4 %convolution_convert_fusion.3 = bf16[2048,1536]{1,0:T(8,128)(2,1)} fusion(bf16[2048,1728]{0,1:T(8,128)(2,1)} %get-tuple-element.147, bf16[1728,1536]{1,0:T(8,128)(2,1)} %param.47), kind=kOutput, calls=%fused_computation.95 | convolution fusion | flops 10874781696 | bytes 18677760 | tf_op jit(solution)/shard_map/dot_general | solution.py:154
  911.8 34.4 %fusion.84 = f32[2,3,512,64]{2,3,1,0:T(8,128)} fusion(f32[2,3,512,1024]{3,2,1,0:T(8,128)} %fusion.220, f32[2,3,512,1024]{3,2,1,0:T(8,128)} %copy-done.11, f32[2,3,512]{2,1,0:T(4,128)} %log_add_fusion.2, pred[512,1024]{1,0:T(8,128)(4,1)} %copy-done.22, bf16[2,2048,64]{1,2,0:T(8,128)(2,1)S(1)} %copy-done.46), kind=kOutput, calls=%fused_computation.99 | convolution fusion | flops 437260288 | bytes 52461568 | tf_op jit(solution)/shard_map/kgqj,kjd->kgqd/dot_general | solution.py:199
  946.3 30.9 %fusion.63 = f32[2,3,512,64]{2,3,1,0:T(8,128)} fusion(f32[2,3,512,1536]{3,2,1,0:T(8,128)} %fusion.217, f32[2,3,512,1536]{3,2,1,0:T(8,128)} %get-tuple-element.165, f32[2,3,512]{2,1,0:T(4,128)S(1)} %copy-done.76, bf16[2,2048,64]{1,2,0:T(8,128)(2,1)S(1)} %copy-done.46), kind=kOutput, calls=%fused_computation.82 | convolution fusion | flops 637014528 | bytes 76709888 | tf_op jit(solution)/shard_map/kgqj,kjd->kgqd/dot_general | solution.py:199
  977.2 45.3 %fusion.27 = f32[2,3,512,64]{2,3,1,0:T(8,128)} fusion(f32[2,3,512,2048]{3,2,1,0:T(8,128)} %fusion.214, f32[2,3,512,2048]{3,2,1,0:T(8,128)} %get-tuple-element.163, f32[2,3,512]{2,1,0:T(4,128)S(1)} %copy-done.78, pred[512,2048]{1,0:T(8,128)(4,1)} %copy-done.20, bf16[2048,2,32]{0,2,1:T(8,128)(2,1)S(1)} %copy-done.40, bf16[2048,2,32]{0,2,1:T(8,128)(2,1)S(1)} %copy-done.37), kind=kOutput, calls=%fused_computation.47 | convolution fusion | flops 875566080 | bytes 52703232 | tf_op jit(solution)/shard_map/kgqj,kjd->kgqd/dot_general | solution.py:199
  1041.2 12.5 add_convert_fusion
  1061.4 40.1 %all-reduce.6 = (f32[64]{0:T(128)}, f32[64]{0:T(128)}) all-reduce(f32[64]{0:T(128)S(1)} %get-tuple-element.129, f32[64]{0:T(128)S(1)} %get-tuple-element.131), channel_id=1, replica_groups=mesh['dp'=8,'tensor'=4] {'dp','tensor'}, use_global_device_ids=true, to_apply=%region_31.32 | all-reduce | flops 128 | bytes 1024 | tf_op jit(solution)/shard_map/psum | solution.py:234
  1101.6 12.7 all-reduce.19.cloned.1.call-done
  1138.5 406.0 %all-reduce.21.cloned.1.call-done = (bf16[2048,1536]{1,0:T(8,128)(2,1)}, bf16[2048,1536]{1,0:T(8,128)(2,1)}) async-done(((bf16[2048,1536]{1,0:T(8,128)(2,1)}, bf16[2048,1536]{1,0:T(8,128)(2,1)}), (bf16[2048,1536]{1,0:T(8,128)(2,1)}, bf16[2048,1536]{1,0:T(8,128)(2,1)})) %all-reduce.21.cloned.1.call-update) | async-done | bytes 12582928 | tf_op jit(solution)/shard_map/psum | solution.py:153
  1552.7 14.8 all-reduce.7
  1568.8 21.0 %fusion.34 = (f32[2048,1536]{1,0:T(8,128)}, bf16[2048,1536]{1,0:T(8,128)(2,1)}) fusion(f32[2048,1536]{1,0:T(8,128)} %copy-done.6, bf16[2048,1536]{1,0:T(8,128)(2,1)} %get-tuple-element.144, bf16[2048,1536]{1,0:T(8,128)(2,1)} %param.34, f32[2048]{0:T(1024)S(1)} %multiply_multiply_fusion.4, f32[1536]{0:T(1024)S(1)} %copy-done.57, f32[2048]{0:T(1024)S(1)} %copy-done.54, ...), kind=kLoop, calls=%fused_computation.53 | loop fusion | flops 40894464 | bytes 56645632 | tf_op jit(solution)/shard_map/add | solution.py:233
  1589.8 15.2 all-gather.3.cloned.1.call-done
  (320 shorter events, 307.7 us)
Async XLA Ops:
  7.2 101.9 %copy-start = (bf16[384,1536]{1,0:T(8,128)(2,1)S(1)}, bf16[384,1536]{1,0:T(8,128)(2,1)}, u32[]{:S(2)}) copy-start(bf16[384,1536]{1,0:T(8,128)(2,1)} %param.41) | copy-start | bytes 3538948
  7.2 333.1 %all-reduce.15.cloned.1.call-start = ((), (), s32[]{:S(2)}) async-start(), calls=%async_computation | async-start | bytes 12582912 | tf_op jit(solution)/shard_map/psum | solution.py:143
  19.2 76.8 %copy-start.12 = (bf16[2048,128]{0,1:T(8,128)(2,1)}, bf16[2048,128]{0,1:T(8,128)(2,1)S(1)}, u32[]{:S(2)}) copy-start(bf16[2048,128]{0,1:T(8,128)(2,1)S(1)} %convolution_convert_fusion.6) | copy-start | bytes 1572868
  27.8 45.7 %copy-start.36 = (bf16[2048,2,32]{0,2,1:T(8,128)(2,1)}, bf16[2048,2,32]{0,2,1:T(8,128)(2,1)S(1)}, u32[]{:S(2)}) copy-start(bf16[2048,2,32]{0,2,1:T(8,128)(2,1)S(1)} %get-tuple-element.156) | copy-start | bytes 786436
  28.9 44.6 %copy-start.28 = (bf16[2048,6,64]{0,2,1:T(8,128)(2,1)}, bf16[2048,6,64]{0,2,1:T(8,128)(2,1)S(1)}, u32[]{:S(2)}) copy-start(bf16[2048,6,64]{0,2,1:T(8,128)(2,1)S(1)} %pad_maximum_fusion.1) | copy-start | bytes 4718596
  114.5 233.2 %copy-start.62 = (f32[1536]{0:T(1024)S(1)}, f32[1536]{0:T(1024)}, u32[]{:S(2)}) copy-start(f32[1536]{0:T(1024)} %param.44) | copy-start | bytes 18436
  114.6 554.0 %all-reduce.17.cloned.1.call-start = ((), (), s32[]{:S(2)}) async-start(), calls=%async_computation.1 | async-start | bytes 12582912 | tf_op jit(solution)/shard_map/psum | solution.py:166
  446.6 667.7 %all-reduce.19.cloned.1.call-start = ((), (), s32[]{:S(2)}) async-start(), calls=%async_computation.3 | async-start | bytes 35782656 | tf_op jit(solution)/shard_map/psum | solution.py:238
  446.7 33.9 %slice-start.7 = ((s8[6291456]{0:T(1024)(128)(4,1)}), s8[4194304]{0:T(1024)(128)(4,1)S(1)}, s32[]{:S(2)}) async-start(s8[6291456]{0:T(1024)(128)(4,1)} %bitcast.204), calls=%async_computation.12 | async-start | bytes 8388608
  480.6 188.0 %copy-start.56 = (f32[2048]{0:T(1024)S(1)}, f32[2048]{0:T(1024)}, u32[]{:S(2)}) copy-start(f32[2048]{0:T(1024)} %copy-done.55) | copy-start | bytes 24580
  480.6 188.0 %copy-start.63 = (f32[1536]{0:T(1024)S(1)}, f32[1536]{0:T(1024)}, u32[]{:S(2)}) copy-start(f32[1536]{0:T(1024)} %param.44) | copy-start | bytes 18436
  493.9 184.9 %copy-start.61 = (f32[2048]{0:T(1024)S(1)}, f32[2048]{0:T(1024)}, u32[]{:S(2)}) copy-start(f32[2048]{0:T(1024)} %copy-done.60) | copy-start | bytes 24580
  825.5 48.9 %copy-start.15 = (f32[2048,32]{0,1:T(8,128)S(1)}, f32[2048,32]{0,1:T(8,128)}, u32[]{:S(2)}) copy-start(f32[2048,32]{0,1:T(8,128)} %copy-done.14) | copy-start | bytes 786436
  825.5 48.9 %copy-start.17 = (f32[2048,32]{0,1:T(8,128)S(1)}, f32[2048,32]{0,1:T(8,128)}, u32[]{:S(2)}) copy-start(f32[2048,32]{0,1:T(8,128)} %copy-done.16) | copy-start | bytes 786436
  825.5 50.2 %copy-start.8 = (f32[2048,128]{0,1:T(8,128)S(1)}, f32[2048,128]{0,1:T(8,128)}, u32[]{:S(2)}) copy-start(f32[2048,128]{0,1:T(8,128)} %copy-done.7) | copy-start | bytes 3145732
  825.5 50.2 %copy-start.50 = (f32[2048,2]{0,1:T(2,128)S(1)}, f32[2048,2]{0,1:T(2,128)}, u32[]{:S(2)}) copy-start(f32[2048,2]{0,1:T(2,128)} %copy-done.49) | copy-start | bytes 49156
  825.5 50.2 %copy-start.84 = (f32[64]{0:T(128)S(1)}, f32[64]{0:T(128)}, u32[]{:S(2)}) copy-start(f32[64]{0:T(128)} %param.43) | copy-start | bytes 772
  825.5 50.6 %copy-start.52 = (f32[2048,2]{0,1:T(2,128)S(1)}, f32[2048,2]{0,1:T(2,128)}, u32[]{:S(2)}) copy-start(f32[2048,2]{0,1:T(2,128)} %copy-done.51) | copy-start | bytes 49156
  881.9 662.6 %all-reduce.21.cloned.1.call-start = ((), (), s32[]{:S(2)}) async-start(), calls=%async_computation.4 | async-start | bytes 25165824 | tf_op jit(solution)/shard_map/psum | solution.py:153
  1053.8 551.2 %all-gather.3.cloned.1.call-start = ((), (), s32[]{:S(2)}) async-start(), calls=%async_computation.2 | async-start | bytes 10616832 | tf_op jit(solution)/shard_map/all_gather | solution.py:237
  1132.8 411.7 %copy-start.54 = (f32[2048]{0:T(1024)S(1)}, f32[2048]{0:T(1024)}, u32[]{:S(2)}) copy-start(f32[2048]{0:T(1024)} %copy-done.53) | copy-start | bytes 24580
  1132.8 411.7 %copy-start.57 = (f32[1536]{0:T(1024)S(1)}, f32[1536]{0:T(1024)}, u32[]{:S(2)}) copy-start(f32[1536]{0:T(1024)} %param.37) | copy-start | bytes 18436
  1138.5 414.2 %copy-start.80 = (bf16[1536]{0:T(1024)(128)(2,1)S(1)}, bf16[1536]{0:T(1024)(128)(2,1)}, u32[]{:S(2)}) copy-start(bf16[1536]{0:T(1024)(128)(2,1)} %get-tuple-element.125) | copy-start | bytes 9220
  1138.5 430.3 %copy-start.59 = (f32[2048]{0:T(1024)S(1)}, f32[2048]{0:T(1024)}, u32[]{:S(2)}) copy-start(f32[2048]{0:T(1024)} %copy-done.58) | copy-start | bytes 24580
  (85 other events, 755.4 us)
Sparse Core Ops, SparseCore 0:
  114.7 225.5 all-reduce.14
  446.7 221.7 all-reduce.16
  882.0 232.2 all-reduce.18
  1117.5 426.9 all-reduce.20
  1547.0 57.9 all-gather.2
